TPU v7x, 128 devices: a whole 4x4x4 slice. The times are simulated.
128 devices in a mesh: slab: 4 (over z_hi, core), wide: 32 (over x, z_lo, y).
Axes of the slice: x: 4, y: 4, z: 4 (z_hi: 2, z_lo: 2; z = z_hi * 2 + z_lo), core: 2. Of those that a mesh axis runs over, the one named last changes fastest.
Arguments:
- orbitals: float32 [256, 128, 128, 128], P(None, 'slab', 'wide'), may hold values from -6 to 6
- points: int32 [512], replicated, may hold values from 0 to 2097151, as said below
Outputs:
- potential: float32 [128, 128, 128, 128], P(None, 'slab', 'wide')
Inputs may be any that keep to these rules, and one draw needn't show every extreme that they name: `points`: the 512 indices are distinct; how many fall in the cells of one device differs strongly between devices.
All inputs are finite; a program needn't handle non-finite values.
Results may differ from a plain program's by a relative error of at most 0.00014.
Values sent between devices are 32-bit elements; how exact they have to be, the bound alone decides.
No kernel may reach another device: no remote copies, remote signals or barrier semaphores. Data moves between devices by JAX's collectives and lax.ppermute only.
A program may use at most 192 MiB of HBM per device.

v0:
```python
import math
import jax
import jax.numpy as jnp
from jax import lax
from jax.sharding import PartitionSpec as P

VEC_DEV = 1
highest = lax.Precision.HIGHEST


def tables(length):
    index = jnp.arange(length, dtype=jnp.int32)
    phase = index[:, None] * index[None, :] % length
    angle = phase.astype(jnp.float32) * (2.0 * math.pi / length)
    return (jnp.cos(angle), jnp.sin(angle))


def contract(values, table, axis_pos):
    letters = "abcd"[: values.ndim]
    target = letters[:axis_pos] + "k" + letters[axis_pos + 1 :]
    return jnp.einsum(
        letters + "," + letters[axis_pos] + "k->" + target, values, table, precision=highest
    )


def rotate(stacked, axis_pos, sign, cosine, sine):
    real_part = stacked[0]
    imag_part = stacked[1]
    new_real = contract(real_part, cosine, axis_pos) - sign * contract(imag_part, sine, axis_pos)
    new_imag = contract(imag_part, cosine, axis_pos) + sign * contract(real_part, sine, axis_pos)
    return jnp.stack([new_real, new_imag])


def coulomb(zfreq, yfreq, xfreq, length, factor):

    def squared(index):
        signed = jnp.where(index > length // 2, index - length, index).astype(jnp.float32) * (
            2.0 * math.pi / length
        )
        return signed * signed

    total = (
        squared(zfreq)[:, None, None]
        + squared(yfreq)[None, :, None]
        + squared(xfreq)[None, None, :]
    )
    safe = jnp.where(total > 0, total, 1.0)
    return jnp.where(total > 0, 4.0 * math.pi * factor / safe, 0.0)


def per_device(orbitals, points):
    norbit, depth, rows, grid = orbitals.shape
    npoint = points.shape[0]
    slab_count = lax.axis_size("slab")
    wide_count = lax.axis_size("wide")
    slab_index = lax.axis_index("slab")
    wide_index = lax.axis_index("wide")
    cells = depth * rows * grid
    flat = orbitals.reshape(norbit, cells)
    zcoord = points // (grid * grid)
    ycoord = points // grid % grid
    xcoord = points % grid
    owned = (zcoord // depth == slab_index) & (ycoord // rows == wide_index)
    offset = ((zcoord - slab_index * depth) * rows + (ycoord - wide_index * rows)) * grid + xcoord
    offset = jnp.where(owned, offset, 0)
    picked = jnp.take(flat, offset, axis=1) * owned.astype(jnp.float32)[None, :]
    sampled = lax.psum(picked, ("slab", "wide"))
    correlation = jnp.dot(sampled.T, sampled, precision=highest)
    gram = correlation * correlation
    gram = gram + 0.01 * jnp.mean(jnp.diagonal(gram)) * jnp.eye(npoint, dtype=jnp.float32)
    factor = jnp.linalg.cholesky(gram)
    devices = slab_count * wide_count
    vectors = VEC_DEV * devices
    coeffs = jax.scipy.linalg.cho_solve((factor, True), jnp.eye(npoint, vectors, dtype=jnp.float32))
    coeff_rows = coeffs.T
    sampled_rows = sampled.T
    width = math.gcd(cells, 4096)

    def fit_block(turn, fitted):
        start = turn * width
        block = lax.dynamic_slice_in_dim(flat, start, width, 1)
        pairs = jnp.dot(sampled_rows, block, precision=highest)
        piece = jnp.dot(coeff_rows, pairs * pairs, precision=highest)
        return lax.dynamic_update_slice_in_dim(fitted, piece, start, 1)

    fitting = lax.fori_loop(0, cells // width, fit_block, jnp.zeros((vectors, cells), jnp.float32))
    cosine, sine = tables(grid)
    scale = 1.0 / float(grid * grid * grid)
    freqs = jnp.arange(grid, dtype=jnp.int32)
    stacked = fitting.reshape(2, vectors // 2, depth, rows, grid)
    spectrum = rotate(stacked, 3, -1.0, cosine, sine)
    spectrum = lax.all_to_all(spectrum, "wide", split_axis=1, concat_axis=3, tiled=True)
    spectrum = rotate(spectrum, 2, -1.0, cosine, sine)
    spectrum = lax.all_to_all(spectrum, "slab", split_axis=3, concat_axis=2, tiled=True)
    spectrum = rotate(spectrum, 1, -1.0, cosine, sine)
    block = grid // slab_count
    kernel = coulomb(
        freqs, slab_index * block + jnp.arange(block, dtype=jnp.int32), freqs, grid, scale
    )
    spectrum = spectrum * kernel
    spectrum = rotate(spectrum, 1, 1.0, cosine, sine)
    spectrum = lax.all_to_all(spectrum, "slab", split_axis=2, concat_axis=3, tiled=True)
    spectrum = rotate(spectrum, 2, 1.0, cosine, sine)
    spectrum = lax.all_to_all(spectrum, "wide", split_axis=3, concat_axis=1, tiled=True)
    spectrum = rotate(spectrum, 3, 1.0, cosine, sine)
    return spectrum.reshape(vectors, depth, rows, grid)


def solution(mesh):
    placed = (P(None, "slab", "wide", None), P())
    return jax.shard_map(
        per_device,
        mesh=mesh,
        in_specs=placed,
        out_specs=P(None, "slab", "wide", None),
        check_vma=False,
    )
```

profile of v0, /device:TPU:0, one launch (start us, length us, event | category | flops | bytes accessed | tf_op | source)
XLA Modules:
  0.0 1024.6 jit_solution(7619435522696950387)
XLA Ops:
  7.3 19.6 %copy.67 = f32[256,32,4,128]{0,3,2,1:T(8,128)} copy(f32[256,32,4,128]{3,2,1,0:T(4,128)} %param.4) | data formatting | bytes 33554432 | tf_op args[0]
  26.9 7.3 gather_fusion
  35.3 148.4 %all-reduce.3.cloned.1.call-done = f32[256,512]{0,1:T(8,128)} async-done(((f32[256,512]{0,1:T(8,128)}), f32[256,512]{0,1:T(8,128)}) %all-reduce.3.cloned.1.call-update) | async-done | bytes 524304 | tf_op jit(solution)/shard_map/psum | solution.py:67
  186.3 5.0 gather_fusion.1
  192.9 11.7 %cholesky.103 = f32[128,128]{1,0:T(8,128)S(1)} custom-call(f32[128,128]{1,0:T(8,128)S(1)} %cholesky.263), custom_call_target="Cholesky" | custom-call | tf_op jit(solution)/shard_map/jit(cholesky)/cholesky | solution.py:71
  204.7 9.8 custom-call.34
  215.2 11.7 %cholesky.215 = f32[128,128]{1,0:T(8,128)S(1)} custom-call(f32[128,128]{1,0:T(8,128)S(1)} %cholesky.267), custom_call_target="Cholesky" | custom-call | tf_op jit(solution)/shard_map/jit(cholesky)/cholesky | solution.py:71
  227.0 9.9 custom-call.35
  237.6 11.7 %cholesky.236 = f32[128,128]{1,0:T(8,128)S(1)} custom-call(f32[128,128]{1,0:T(8,128)S(1)} %cholesky.272), custom_call_target="Cholesky" | custom-call | tf_op jit(solution)/shard_map/jit(cholesky)/cholesky | solution.py:71
  250.0 9.8 custom-call.36
  260.5 11.7 %cholesky.253 = f32[128,128]{1,0:T(8,128)S(1)} custom-call(f32[128,128]{1,0:T(8,128)S(1)} %convolution_subtract_fusion.8), custom_call_target="Cholesky" | custom-call | tf_op jit(solution)/shard_map/jit(cholesky)/cholesky | solution.py:71
  276.3 10.6 %while.15 = (s32[]{:T(128)}, f32[512,512]{1,0:T(8,128)S(1)}, s32[4,2]{0,1:T(2,128)S(1)}, f32[4,128,128]{2,1,0:T(8,128)}, s32[]{:T(128)}) while((s32[]{:T(128)}, f32[512,512]{1,0:T(8,128)S(1)}, s32[4,2]{0,1:T(2,128)S(1)}, f32[4,128,128]{2,1,0:T(8,128)}, s32[]{:T(128)}) %tuple.60), condition=%wide.while_cond, body=%wide.while_body.sunk | while | flops 2 | bytes 132705 | solution.py:74
  286.8 40.3 %custom-call.37 = f32[4,128,128]{1,2,0:T(8,128)S(1)} custom-call(f32[4,128,128]{2,1,0:T(8,128)} %get-tuple-element.107), custom_call_target="InvertDiagBlocksLowerTriangular" | custom-call | tf_op jit(solution)/shard_map/jit(_cho_solve)/triangular_solve | solution.py:74
  335.0 68.7 %while.14 = (s32[]{:T(128)}, f32[128,16384]{0,1:T(8,128)}, f32[256,16384]{0,1:T(8,128)}, f32[512,256]{1,0:T(8,128)S(1)}, f32[128,512]{1,0:T(8,128)S(1)}, /*index=5*/s32[]{:T(128)}, s32[]{:T(128)}, s32[]{:T(128)}, s32[]{:T(128)}) while((s32[]{:T(128)}, f32[128,16384]{0,1:T(8,128)}, f32[256,16384]{0,1:T(8,128)}, f32[512,256]{1,0:T(8,128)S(1)}, ...), condition=%wide.region_11.12_spmd, body=%wide.region_10.11_spmd.sunk | while | flops 9665773568 | bytes 23855252 | solution.py:86
  335.0 9.1 fusion.295
  344.1 8.1 fusion.296
  352.2 9.1 fusion.295
  361.3 8.1 fusion.296
  369.3 9.1 fusion.295
  378.4 8.1 fusion.296
  386.5 9.1 fusion.295
  395.6 8.1 fusion.296
  403.7 13.2 %fusion.249 = (f32[64,16384]{0,1:T(8,128)}, f32[64,16384]{0,1:T(8,128)}) fusion(f32[128,16384]{0,1:T(8,128)} %get-tuple-element.99), kind=kLoop, calls=%fused_computation.325 | loop fusion | bytes 16777216 | tf_op jit(solution)/shard_map/slice | solution.py:27
  416.9 7.3 copy.72
  424.2 7.1 fusion.79
  431.3 7.3 copy.74
  438.7 7.4 fusion.77
  457.7 101.2 %all_to_all.60 = f32[2,64,32,4,128]{4,2,3,0,1:T(8,128)} all-to-all(f32[2,64,32,4,128]{4,2,3,0,1:T(8,128)S(1)} %copy.77), channel_id=1, replica_groups=mesh['slab'=4,'wide'=32] {'wide'}, dimensions={1} | all-to-all | bytes 16777216 | tf_op jit(solution)/shard_map/all_to_all | solution.py:92
  558.9 12.2 %copy.150 = f32[2,32,2,32,4,128]{5,4,1,3,2,0:T(4,128)} copy(f32[2,32,2,32,4,128]{5,3,4,0,2,1:T(8,128)} %bitcast.268) | data formatting | bytes 16777216 | tf_op jit(solution)/shard_map/all_to_all | solution.py:92
  579.2 4.5 fusion.71
  593.3 8.4 copy.83
  601.8 5.7 all-to-all-start.1
  608.2 93.9 %all-to-all-done.1 = f32[2,2,32,128,128]{4,2,1,0,3:T(8,128)} async-done(((f32[2,2,32,128,128]{4,2,1,0,3:T(8,128)}), f32[2,2,32,128,128]{4,2,1,0,3:T(8,128)}, u32[]{:S(2)}, u32[]{:S(2)}) %all-to-all-start.1) | async-done | bytes 8388640 | tf_op jit(solution)/shard_map/all_to_all | solution.py:94
  702.1 4.4 copy.149
  716.5 5.1 subtract_bitcast_fusion.3
  721.7 4.7 add_bitcast_fusion.3
  727.9 4.4 fusion.12
  732.3 4.4 fusion.11
  736.7 4.6 subtract_bitcast_fusion.2
  741.3 4.4 add_bitcast_fusion.2
  746.9 4.9 copy.93
  751.7 97.3 %all_to_all.61 = f32[2,2,128,32,128]{4,3,1,0,2:T(8,128)S(1)} all-to-all(f32[2,2,128,32,128]{4,3,1,0,2:T(8,128)S(1)} %copy.93), channel_id=1, replica_groups=mesh['slab'=4,'wide'=32] {'slab'}, dimensions={2} | all-to-all | bytes 16777216 | tf_op jit(solution)/shard_map/all_to_all | solution.py:102
  860.6 4.7 subtract_bitcast_fusion.1
  865.3 4.5 add_bitcast_fusion.1
  870.9 5.3 copy.99
  876.2 102.6 %all_to_all.62 = f32[2,2,32,128,128]{4,2,1,0,3:T(8,128)S(1)} all-to-all(f32[2,2,32,128,128]{4,2,1,0,3:T(8,128)S(1)} %copy.99), channel_id=1, replica_groups=mesh['slab'=4,'wide'=32] {'wide'}, dimensions={3} | all-to-all | bytes 16777216 | tf_op jit(solution)/shard_map/all_to_all | solution.py:104
  998.0 4.3 pad_maximum_fusion.4
  1002.3 15.2 %copy.101 = f32[128,32,4,128]{3,2,1,0:T(4,128)} copy(f32[128,32,4,128]{3,1,2,0:T(8,128)} %bitcast.267) | data formatting | bytes 16777216 | tf_op jit(solution)/shard_map/reshape | solution.py:106
  (100 shorter events, 102.1 us)
Async XLA Ops:
  6.5 177.2 %all-reduce.3.cloned.1.call-start = ((), (), s32[]{:S(2)}) async-start(), calls=%async_computation.4 | async-start | bytes 1048576 | tf_op jit(solution)/shard_map/psum | solution.py:67
  331.3 3.7 copy-start.2
  438.6 7.4 copy-start.1
  438.7 7.4 copy-start.3
  446.0 4.0 copy-start
  601.8 100.3 %all-to-all-start.1 = ((f32[2,2,32,128,128]{4,2,1,0,3:T(8,128)}), f32[2,2,32,128,128]{4,2,1,0,3:T(8,128)}, u32[]{:S(2)}, u32[]{:S(2)}) async-start(f32[2,2,32,128,128]{4,2,1,0,3:T(8,128)} %copy.83), calls=%async_computation.1 | async-start | bytes 16777216 | tf_op jit(solution)/shard_map/all_to_all | solution.py:94
Sparse Core Ops, SparseCore 0:
  35.3 148.3 all-reduce.2
where the time goes:
time: 1030 us; the launch traced here: 1020 us
  blocking collectives  301 us (29%)
  waiting for transfers between devices  242 us (23%)
  matrix products  185 us (18%)
  local copies, waits for them, and re-layouts  139 us (13%)
  other arithmetic  133 us (13%)
  between operations  17.5 us (2%)
    psum x1, waiting for transfers between devices, per_device(): sampled = lax.psum(picked, ('slab', 'wide'))  148 us
    dot_general x24, matrix products, contract(): jnp.einsum(letters + ',' + letters[axis_pos] + 'k->' + target, values, ta...  109 us
    all_to_all x1, blocking collectives, per_device(): lax.all_to_all(spectrum, 'wide', split_axis=3, concat_axis=1, tiled=True)  103 us
    all_to_all x1, blocking collectives, per_device(): lax.all_to_all(spectrum, 'wide', split_axis=1, concat_axis=3, tiled=True)  101 us
    all_to_all x1, blocking collectives, per_device(): lax.all_to_all(spectrum, 'slab', split_axis=2, concat_axis=3, tiled=True)  97.3 us
    all_to_all x1, waiting for transfers between devices, per_device(): lax.all_to_all(spectrum, 'slab', split_axis=3, concat_axis=2, tiled=True)  93.9 us
    another operation x14, other arithmetic, per_device(): factor = jnp.linalg.cholesky(gram)  78.6 us
    another operation x3, other arithmetic, per_device(): jax.scipy.linalg.cho_solve((factor, True), jnp.eye(npoint, vectors, dtype...  40.4 us
  transfers between devices with their start and end apart: 2, of which 2 were waited for; matrix products, arithmetic and copies ran while one was open for 0% of the time, Pallas kernels for 0%

commit v1 on v0

--- a/solution.py
+++ b/solution.py
@@ -64,7 +64,7 @@
     offset = ((zcoord - slab_index * depth) * rows + (ycoord - wide_index * rows)) * grid + xcoord
     offset = jnp.where(owned, offset, 0)
     picked = jnp.take(flat, offset, axis=1) * owned.astype(jnp.float32)[None, :]
-    sampled = lax.psum(picked, ("slab", "wide"))
+    sampled = jnp.sum(lax.all_gather(picked, ("slab", "wide")), axis=0)
     correlation = jnp.dot(sampled.T, sampled, precision=highest)
     gram = correlation * correlation
     gram = gram + 0.01 * jnp.mean(jnp.diagonal(gram)) * jnp.eye(npoint, dtype=jnp.float32)

time: 1030 us -> 1290 us (1.25)
  waiting for transfers between devices: 242 us -> 480 us
  other arithmetic: 133 us -> 153 us
    all_gather x0 -> x1, waiting for transfers between devices: none -> 386 us  [per_device(): sampled = jnp.sum(lax.all_gather(picked, ('slab', 'wide')), axis=0)]
    psum x1 -> x0, waiting for transfers between devices: 148 us -> none  [per_device(): sampled = lax.psum(picked, ('slab', 'wide'))]
    reduce_sum x0 -> x1, other arithmetic: none -> 20.9 us  [per_device(): sampled = jnp.sum(lax.all_gather(picked, ('slab', 'wide')), axis=0)]
where the time goes in v1:
time: 1290 us; the launch traced here: 1280 us
  waiting for transfers between devices  480 us (37%)
  blocking collectives  300 us (23%)
  matrix products  188 us (15%)
  other arithmetic  153 us (12%)
  local copies, waits for them, and re-layouts  139 us (11%)
  between operations  17.5 us (1%)
    all_gather x1, waiting for transfers between devices, per_device(): sampled = jnp.sum(lax.all_gather(picked, ('slab', 'wide')), axis=0)  386 us
    dot_general x24, matrix products, contract(): jnp.einsum(letters + ',' + letters[axis_pos] + 'k->' + target, values, ta...  109 us
    all_to_all x1, blocking collectives, per_device(): lax.all_to_all(spectrum, 'wide', split_axis=1, concat_axis=3, tiled=True)  103 us
    all_to_all x1, blocking collectives, per_device(): lax.all_to_all(spectrum, 'wide', split_axis=3, concat_axis=1, tiled=True)  99.2 us
    all_to_all x1, blocking collectives, per_device(): lax.all_to_all(spectrum, 'slab', split_axis=2, concat_axis=3, tiled=True)  97.3 us
    all_to_all x1, waiting for transfers between devices, per_device(): lax.all_to_all(spectrum, 'slab', split_axis=3, concat_axis=2, tiled=True)  93.9 us
    another operation x14, other arithmetic, per_device(): factor = jnp.linalg.cholesky(gram)  78.6 us
    another operation x3, other arithmetic, per_device(): jax.scipy.linalg.cho_solve((factor, True), jnp.eye(npoint, vectors, dtype...  39.7 us
  transfers between devices with their start and end apart: 2, of which 2 were waited for; matrix products, arithmetic and copies ran while one was open for 0% of the time, Pallas kernels for 0%

profile of v1, /device:TPU:0, one launch (start us, length us, event | category | flops | bytes accessed | tf_op | source)
XLA Modules:
  0.0 1281.8 jit_solution(2659419984308550883)
XLA Ops:
  7.3 19.6 %copy.103 = f32[256,32,4,128]{0,3,2,1:T(8,128)} copy(f32[256,32,4,128]{3,2,1,0:T(4,128)} %param.4) | data formatting | bytes 33554432 | tf_op args[0]
  26.8 7.3 gather_fusion
  35.5 385.8 %all-gather.2.cloned.1.call-done = f32[128,256,512]{2,1,0:T(8,128)} async-done(((f32[1,256,512]{2,1,0:T(8,128)}), f32[128,256,512]{2,1,0:T(8,128)}) %all-gather.2.cloned.1.call-update) | async-done | bytes 67108880 | tf_op jit(solution)/shard_map/all_gather | solution.py:67
  421.2 20.9 %reduce_sum.18 = f32[256,512]{1,0:T(8,128)S(1)} reduce(f32[128,256,512]{2,1,0:T(8,128)} %all-gather.2.cloned.1.call-done, f32[]{:T(128)} %constant.289.clone.1), dimensions={0}, to_apply=%region_0.1 | reduce | flops 16646144 | bytes 67633152 | tf_op jit(solution)/shard_map/reduce_sum | solution.py:67
  443.5 5.0 gather_fusion.1
  451.0 11.7 cholesky.103
  462.9 9.8 custom-call.34
  475.2 11.7 cholesky.215
  487.0 10.0 custom-call.35
  498.5 11.7 cholesky.236
  511.0 9.8 custom-call.36
  522.2 11.7 cholesky.253
  538.0 8.5 while.15
  546.5 39.5 %custom-call.37 = f32[4,128,128]{1,2,0:T(8,128)S(1)} custom-call(f32[4,128,128]{2,1,0:T(8,128)S(1)} %get-tuple-element.107), custom_call_target="InvertDiagBlocksLowerTriangular" | custom-call | tf_op jit(solution)/shard_map/jit(_cho_solve)/triangular_solve | solution.py:74
  594.0 68.7 %while.14 = (s32[]{:T(128)}, f32[128,16384]{0,1:T(8,128)}, f32[256,16384]{0,1:T(8,128)}, f32[512,256]{1,0:T(8,128)S(1)}, f32[128,512]{1,0:T(8,128)S(1)}, /*index=5*/s32[]{:T(128)}, s32[]{:T(128)}, s32[]{:T(128)}, s32[]{:T(128)}) while((s32[]{:T(128)}, f32[128,16384]{0,1:T(8,128)}, f32[256,16384]{0,1:T(8,128)}, f32[512,256]{1,0:T(8,128)S(1)}, ...), condition=%wide.region_11.12_spmd, body=%wide.region_10.11_spmd.sunk | while | flops 9665773568 | bytes 23855252 | solution.py:86
  594.0 9.1 fusion.296
  603.1 8.1 fusion.297
  611.2 9.1 fusion.296
  620.3 8.1 fusion.297
  628.4 9.1 fusion.296
  637.5 8.1 fusion.297
  645.5 9.1 fusion.296
  654.6 8.1 fusion.297
  662.7 13.1 %fusion.250 = (f32[64,16384]{0,1:T(8,128)}, f32[64,16384]{0,1:T(8,128)}) fusion(f32[128,16384]{0,1:T(8,128)} %get-tuple-element.99), kind=kLoop, calls=%fused_computation.326 | loop fusion | bytes 16777216 | tf_op jit(solution)/shard_map/slice | solution.py:27
  675.8 7.3 copy.110
  683.2 7.1 fusion.80
  690.3 7.3 copy.112
  697.6 7.3 fusion.78
  716.6 103.0 %all_to_all.60 = f32[2,64,32,4,128]{4,2,3,0,1:T(8,128)} all-to-all(f32[2,64,32,4,128]{4,2,3,0,1:T(8,128)S(1)} %copy.115), channel_id=1, replica_groups=mesh['slab'=4,'wide'=32] {'wide'}, dimensions={1} | all-to-all | bytes 16777216 | tf_op jit(solution)/shard_map/all_to_all | solution.py:92
  819.6 12.2 copy.188
  839.9 4.5 fusion.72
  854.1 8.4 copy.121
  862.5 5.7 all-to-all-start.1
  868.9 93.9 %all-to-all-done.1 = f32[2,2,32,128,128]{4,2,1,0,3:T(8,128)} async-done(((f32[2,2,32,128,128]{4,2,1,0,3:T(8,128)}), f32[2,2,32,128,128]{4,2,1,0,3:T(8,128)}, u32[]{:S(2)}, u32[]{:S(2)}) %all-to-all-start.1) | async-done | bytes 8388640 | tf_op jit(solution)/shard_map/all_to_all | solution.py:94
  962.8 4.4 copy.187
  977.3 5.1 subtract_bitcast_fusion.3
  982.4 4.7 add_bitcast_fusion.3
  988.6 4.4 fusion.12
  993.0 4.4 fusion.11
  997.4 4.6 subtract_bitcast_fusion.2
  1002.1 4.4 add_bitcast_fusion.2
  1007.6 4.9 copy.131
  1012.5 97.3 %all_to_all.61 = f32[2,2,128,32,128]{4,3,1,0,2:T(8,128)S(1)} all-to-all(f32[2,2,128,32,128]{4,3,1,0,2:T(8,128)S(1)} %copy.131), channel_id=1, replica_groups=mesh['slab'=4,'wide'=32] {'slab'}, dimensions={2} | all-to-all | bytes 16777216 | tf_op jit(solution)/shard_map/all_to_all | solution.py:102
  1121.3 4.7 subtract_bitcast_fusion.1
  1126.0 4.5 add_bitcast_fusion.1
  1131.6 5.3 copy.137
  1136.9 99.2 %all_to_all.62 = f32[2,2,32,128,128]{4,2,1,0,3:T(8,128)S(1)} all-to-all(f32[2,2,32,128,128]{4,2,1,0,3:T(8,128)S(1)} %copy.137), channel_id=1, replica_groups=mesh['slab'=4,'wide'=32] {'wide'}, dimensions={3} | all-to-all | bytes 16777216 | tf_op jit(solution)/shard_map/all_to_all | solution.py:104
  1259.5 15.2 %copy.139 = f32[128,32,4,128]{3,2,1,0:T(4,128)} copy(f32[128,32,4,128]{3,1,2,0:T(8,128)} %bitcast.271) | data formatting | bytes 16777216 | tf_op jit(solution)/shard_map/reshape | solution.py:106
  (103 shorter events, 108.0 us)
Async XLA Ops:
  6.5 414.7 %all-gather.2.cloned.1.call-start = ((), (), s32[]{:S(2)}) async-start(), calls=%async_computation.4 | async-start | bytes 67633152 | tf_op jit(solution)/shard_map/all_gather | solution.py:67
  450.0 1.0 copy-start.3
  697.6 7.4 copy-start.1
  697.6 7.4 copy-start.2
  704.9 4.0 copy-start
  862.5 100.3 %all-to-all-start.1 = ((f32[2,2,32,128,128]{4,2,1,0,3:T(8,128)}), f32[2,2,32,128,128]{4,2,1,0,3:T(8,128)}, u32[]{:S(2)}, u32[]{:S(2)}) async-start(f32[2,2,32,128,128]{4,2,1,0,3:T(8,128)} %copy.121), calls=%async_computation.1 | async-start | bytes 16777216 | tf_op jit(solution)/shard_map/all_to_all | solution.py:94
Sparse Core Ops, SparseCore 0:
  35.5 385.6 all-gather.1
